TPU v7x, 256 devices: a whole 4x4x8 slice. The times are simulated.
256 devices in a mesh: tiles: 16 (over y, z_lo, core), coef: 16 (over x, z_hi).
Axes of the slice: x: 4, y: 4, z: 8 (z_hi: 4, z_lo: 2; z = z_hi * 2 + z_lo), core: 2. Of those that a mesh axis runs over, the one named last changes fastest.
Arguments:
- fields: bfloat16 [256, 8192], P('coef', 'tiles'), may hold values from -6 to 6
- adjoints: bfloat16 [256, 8192], P('coef', 'tiles'), may hold values from -6 to 6
- couple: bfloat16 [30, 256, 256], replicated, may hold values from -0.0625 to 0.0625
- tmatrices: bfloat16 [64, 256, 256], P('tiles', 'coef'), may hold values from -0.375 to 0.375
- neighbours: int32 [8192, 30], P('tiles'), may hold values from -1 to 8191, as said below
- classes: int32 [8192], P('tiles'), may hold values from 0 to 63
Outputs:
- forward_out: bfloat16 [256, 8192], P('coef', 'tiles')
- adjoint_out: bfloat16 [256, 8192], P('coef', 'tiles')
Inputs may be any that keep to these rules, and one draw needn't show every extreme that they name: neighbours[i, m] is -1 or i + m - 15 for m < 15, or i + m - 14 for m >= 15; links are mutual: neighbours[i, m] = j >= 0 exactly when neighbours[j, 29 - m] = i; slots 15 - 1 and 15 are filled wherever the neighbouring pillar exists.
All inputs are finite; a program needn't handle non-finite values.
Results may differ from a plain program's by a relative error of at most 0.0037.
Values may be sent and summed in bfloat16 or wider, within the bound.
A program may use at most 64 MiB of HBM per device.

v0:
```python
import jax
import jax.numpy as jnp
from jax import lax
from jax.sharding import PartitionSpec as P

SLOTS = 30
HW = 15


def padded_2(cells, sides, width):
    for axis, dim in sides:
        count = lax.axis_size(axis)
        ends = count - 1
        head = lax.slice_in_dim(cells, 0, width, axis=dim)
        tail = lax.slice_in_dim(cells, cells.shape[dim] - width, cells.shape[dim], axis=dim)
        cells = jnp.concatenate(
            [
                lax.ppermute(tail, axis, [(i, (i + 1) % count) for i in range(ends)]),
                cells,
                lax.ppermute(head, axis, [((i + 1) % count, i) for i in range(ends)]),
            ],
            axis=dim,
        )
    return cells


def slot_columns(padded, weight_table, starts, width):
    pieces = [
        padded[:, start : start + width] * weight_table[slot][None, :]
        for slot, start in enumerate(starts)
    ]
    return jnp.stack(pieces, axis=1)


def local(fields, adjoints, couple, tmatrices, neighbours, classes):
    row_count = fields.shape[0]
    tile_len = fields.shape[1]
    coef_index = lax.axis_index("coef")
    is_valid = neighbours >= 0
    slot_weight = is_valid.astype(jnp.bfloat16).T
    forward_starts = [slot + (1 if slot >= HW else 0) for slot in range(SLOTS)]
    adjoint_starts = forward_starts[::-1]
    own_first = coef_index * row_count

    def translate(source, weight_table, starts, adjoint_mode):
        padded = padded_2(source, (("tiles", 1),), HW)
        own_mats = lax.dynamic_slice_in_dim(couple, own_first, row_count, 2 if adjoint_mode else 1)

        def add_piece(arrived):
            selected = slot_columns(arrived, weight_table, starts, tile_len)
            if adjoint_mode:
                block_mat = own_mats
                return jnp.einsum(
                    "nkr,kni->ri", block_mat, selected, preferred_element_type=jnp.float32
                )
            block_mat = own_mats
            return jnp.einsum(
                "nrk,kni->ri", block_mat, selected, preferred_element_type=jnp.float32
            )

        return add_piece(lax.all_gather(padded, "coef", axis=0, tiled=True))

    coupled = translate(fields, slot_weight, forward_starts, False).astype(jnp.bfloat16)
    class_rows = lax.all_gather(tmatrices, "tiles", axis=0, tiled=True)
    sub_table = class_rows
    picked = jnp.take(sub_table, classes, axis=0)
    applied = jnp.einsum(
        "irk,ki->ri",
        picked,
        lax.all_gather(coupled, "coef", axis=0, tiled=True),
        preferred_element_type=jnp.float32,
    )
    forward_out = (fields.astype(jnp.float32) - applied).astype(jnp.bfloat16)
    class_cols = lax.all_to_all(class_rows, "coef", split_axis=2, concat_axis=1, tiled=True)
    sub_table = class_cols
    picked = jnp.take(sub_table, classes, axis=0)
    scattered_sum = jnp.einsum(
        "irk,ri->ki",
        picked,
        lax.all_gather(adjoints, "coef", axis=0, tiled=True),
        preferred_element_type=jnp.float32,
    )
    scattered = scattered_sum.astype(jnp.bfloat16)
    returned = translate(scattered, slot_weight[::-1], adjoint_starts, True)
    adjoint_out = (adjoints.astype(jnp.float32) - returned).astype(jnp.bfloat16)
    return (forward_out, adjoint_out)


def solution(mesh):
    placed = (
        P("coef", "tiles"),
        P("coef", "tiles"),
        P(),
        P("tiles", "coef", None),
        P("tiles", None),
        P("tiles"),
    )
    return jax.shard_map(
        local,
        mesh=mesh,
        in_specs=placed,
        out_specs=(P("coef", "tiles"), P("coef", "tiles")),
        check_vma=False,
    )
```

profile of v0, /device:TPU:32, one launch (start us, length us, event | category | flops | bytes accessed | tf_op | source)
XLA Modules:
  0.0 260.7 jit_solution(10606946548636086392)
XLA Ops:
  0.6 0.8 fusion.138
  1.5 1.9 collective-permute-start
  3.4 3.6 %collective-permute-start.1 = (bf16[16,15]{1,0:T(8,128)(2,1)S(1)}, bf16[16,15]{1,0:T(8,128)(2,1)S(1)}, u32[]{:S(2)}, u32[]{:S(2)}) collective-permute-start(bf16[16,15]{1,0:T(8,128)(2,1)S(1)} %get-tuple-element.37), channel_id=1, source_target_pairs={{16,0},{32,16},{48,32},{64,48},{80,64},{96,80},{112,96},{128,112},... | collective-permute-start | bytes 1448 | tf_op jit(solution)/shard_map/ppermute | solution.py:20
  7.0 19.3 %all_gather.17 = bf16[64,16,256]{2,1,0:T(8,128)(2,1)S(1)} all-gather(bf16[4,16,256]{2,1,0:T(8,128)(2,1)} %param.9), channel_id=1, replica_groups=mesh['tiles'=16,'coef'=16] {'tiles'}, dimensions={0}, use_global_device_ids=true | all-gather | bytes 557056 | tf_op jit(solution)/shard_map/all_gather | solution.py:64
  26.3 1.3 copy.22
  27.6 1.5 reshape.63
  29.1 11.2 %all-to-all-start = ((bf16[16,2,8192]{2,1,0:T(2,128)(2,1)}), bf16[16,2,8192]{2,1,0:T(2,128)(2,1)S(1)}, u32[]{:S(2)}, u32[]{:S(2)}) async-start(bf16[16,2,8192]{2,1,0:T(2,128)(2,1)} %reshape.63), calls=%async_computation | async-start | bytes 1048576 | tf_op jit(solution)/shard_map/all_to_all | solution.py:74
  40.3 0.8 fusion.133
  41.4 0.7 compare_select_fusion
  42.1 0.7 compare_and_fusion
  42.8 50.0 %all_gather.18 = bf16[256,512]{1,0:T(8,128)(2,1)S(1)} all-gather(bf16[16,512]{1,0:T(8,128)(2,1)} %param.7), channel_id=1, replica_groups=mesh['tiles'=16,'coef'=16] {'coef'}, dimensions={0}, use_global_device_ids=true | all-gather | bytes 278528 | tf_op jit(solution)/shard_map/all_gather | solution.py:80
  92.8 3.4 %gather_fusion = bf16[512,16,256]{2,1,0:T(8,128)(2,1)} fusion(bf16[64,16,256]{2,1,0:T(8,128)(2,1)S(1)} %all_gather.17, s32[1024]{0:T(1024)S(1)} %pad_clamp_fusion), kind=kCustom, calls=%fused_computation | custom fusion | bytes 8390656 | tf_op jit(solution)/shard_map/jit(_take)/gather | solution.py:66
  96.2 0.2 copy.40
  96.5 42.1 %all_gather.15 = bf16[256,542]{1,0:T(8,128)(2,1)S(1)} all-gather(bf16[16,542]{1,0:T(8,128)(2,1)S(1)} %pad_maximum_fusion), channel_id=1, replica_groups=mesh['tiles'=16,'coef'=16] {'coef'}, dimensions={0}, use_global_device_ids=true | all-gather | bytes 294848 | tf_op jit(solution)/shard_map/all_gather | solution.py:61
  138.7 0.1 fusion.129
  138.9 0.1 fusion.127
  139.2 0.1 fusion.123
  139.5 0.1 fusion.119
  143.0 2.1 fusion.8
  145.1 40.5 %all_gather.16 = bf16[256,512]{1,0:T(8,128)(2,1)S(1)} all-gather(bf16[16,512]{1,0:T(8,128)(2,1)S(1)} %fusion.8), channel_id=1, replica_groups=mesh['tiles'=16,'coef'=16] {'coef'}, dimensions={0}, use_global_device_ids=true | all-gather | bytes 278528 | tf_op jit(solution)/shard_map/all_gather | solution.py:70
  185.6 0.2 copy.39
  185.9 0.7 reshape.64
  186.5 0.3 copy.24
  186.8 1.3 copy.25
  188.1 3.5 %gather_fusion.1 = bf16[512,256,16]{1,2,0:T(8,128)(2,1)} fusion(bf16[64,256,16]{1,2,0:T(8,128)(2,1)S(1)} %copy.25, s32[1024]{0:T(1024)S(1)} %pad_clamp_fusion), kind=kCustom, calls=%fused_computation.1 | custom fusion | bytes 8390656 | tf_op jit(solution)/shard_map/jit(_take)/gather | solution.py:76
  191.6 13.6 %multiply_reduce_fusion = (bf16[512,16]{1,0:T(8,128)(2,1)S(1)}, f32[512,16]{1,0:T(8,128)S(1)}) fusion(f32[512,256]{1,0:T(8,128)S(1)} %copy.40, bf16[512,256,16]{1,2,0:T(8,128)(2,1)} %gather_fusion.1, pred[512]{0:T(512)(128)(4,1)S(1)} %compare_and_fusion, bf16[512,16,256]{2,1,0:T(8,128)(2,1)} %gather_fusion, f32[512,256]{1,0:T(8,128)S(1)} %copy.39), kind=kLoop, calls=%fused_computation.2 | loop fusion | flops 16760832 | bytes 9486848
  205.4 1.9 collective-permute-start.2
  207.3 3.6 %collective-permute-start.3 = (bf16[16,15]{1,0:T(8,128)(2,1)S(1)}, bf16[16,15]{1,0:T(8,128)(2,1)S(1)}, u32[]{:S(2)}, u32[]{:S(2)}) collective-permute-start(bf16[16,15]{1,0:T(8,128)(2,1)S(1)} %get-tuple-element.35), channel_id=1, source_target_pairs={{16,0},{32,16},{48,32},{64,48},{80,64},{96,80},{112,96},{128,112},... | collective-permute-start | bytes 1448 | tf_op jit(solution)/shard_map/ppermute | solution.py:20
  211.0 0.6 fusion.134
  211.7 0.6 collective-permute-done.3
  212.3 41.8 %all_gather.19 = bf16[256,542]{1,0:T(8,128)(2,1)S(1)} all-gather(bf16[16,542]{1,0:T(8,128)(2,1)S(1)} %pad_maximum_fusion.1), channel_id=1, replica_groups=mesh['tiles'=16,'coef'=16] {'coef'}, dimensions={0}, use_global_device_ids=true | all-gather | bytes 294848 | tf_op jit(solution)/shard_map/all_gather | solution.py:61
  258.5 2.2 fusion.9
  (76 shorter events, 8.4 us)
Async XLA Ops:
  0.6 95.8 %copy-start.1 = (bf16[16,512]{1,0:T(8,128)(2,1)S(1)}, bf16[16,512]{1,0:T(8,128)(2,1)}, u32[]{:S(2)}) copy-start(bf16[16,512]{1,0:T(8,128)(2,1)} %param.6) | copy-start | bytes 49156
  1.5 95.0 %collective-permute-start = (bf16[16,15]{1,0:T(8,128)(2,1)S(1)}, bf16[16,15]{1,0:T(8,128)(2,1)S(1)}, u32[]{:S(2)}, u32[]{:S(2)}) collective-permute-start(bf16[16,15]{1,0:T(8,128)(2,1)S(1)} %get-tuple-element.36), channel_id=1, source_target_pairs={{0,16},{16,32},{32,48},{48,64},{64,80},{80,96},{96,112},{112,128},... | collective-permute-start | bytes 1448 | tf_op jit(solution)/shard_map/ppermute | solution.py:18
  3.4 93.1 %collective-permute-start.1 = (bf16[16,15]{1,0:T(8,128)(2,1)S(1)}, bf16[16,15]{1,0:T(8,128)(2,1)S(1)}, u32[]{:S(2)}, u32[]{:S(2)}) collective-permute-start(bf16[16,15]{1,0:T(8,128)(2,1)S(1)} %get-tuple-element.37), channel_id=1, source_target_pairs={{16,0},{32,16},{48,32},{64,48},{80,64},{96,80},{112,96},{128,112},... | collective-permute-start | bytes 1448 | tf_op jit(solution)/shard_map/ppermute | solution.py:20
  29.1 156.7 %all-to-all-start = ((bf16[16,2,8192]{2,1,0:T(2,128)(2,1)}), bf16[16,2,8192]{2,1,0:T(2,128)(2,1)S(1)}, u32[]{:S(2)}, u32[]{:S(2)}) async-start(bf16[16,2,8192]{2,1,0:T(2,128)(2,1)} %reshape.63), calls=%async_computation | async-start | bytes 1048576 | tf_op jit(solution)/shard_map/all_to_all | solution.py:74
  205.4 6.3 %collective-permute-start.2 = (bf16[16,15]{1,0:T(8,128)(2,1)S(1)}, bf16[16,15]{1,0:T(8,128)(2,1)S(1)}, u32[]{:S(2)}, u32[]{:S(2)}) collective-permute-start(bf16[16,15]{1,0:T(8,128)(2,1)S(1)} %get-tuple-element.34), channel_id=1, source_target_pairs={{0,16},{16,32},{32,48},{48,64},{64,80},{80,96},{96,112},{112,128},... | collective-permute-start | bytes 1448 | tf_op jit(solution)/shard_map/ppermute | solution.py:18
  207.3 5.0 %collective-permute-start.3 = (bf16[16,15]{1,0:T(8,128)(2,1)S(1)}, bf16[16,15]{1,0:T(8,128)(2,1)S(1)}, u32[]{:S(2)}, u32[]{:S(2)}) collective-permute-start(bf16[16,15]{1,0:T(8,128)(2,1)S(1)} %get-tuple-element.35), channel_id=1, source_target_pairs={{16,0},{32,16},{48,32},{64,48},{80,64},{96,80},{112,96},{128,112},... | collective-permute-start | bytes 1448 | tf_op jit(solution)/shard_map/ppermute | solution.py:20
  254.2 4.3 %copy-start = (bf16[30,256,256]{2,1,0:T(8,128)(2,1)S(1)}, bf16[30,256,256]{2,1,0:T(8,128)(2,1)}, u32[]{:S(2)}) copy-start(bf16[30,256,256]{2,1,0:T(8,128)(2,1)} %param.8) | copy-start | bytes 11796484
  254.2 4.3 %copy-start.2 = (bf16[16,512]{1,0:T(8,128)(2,1)S(1)}, bf16[16,512]{1,0:T(8,128)(2,1)}, u32[]{:S(2)}) copy-start(bf16[16,512]{1,0:T(8,128)(2,1)} %param.7) | copy-start | bytes 49156
where the time goes:
time: 261 us
  blocking collectives  194 us (74%)
  other arithmetic  24.9 us (10%)
  starting transfers between devices  22.3 us (9%)
  local copies, waits for them, and re-layouts  13.7 us (5%)
  matrix products  4.25 us (2%)
    all_gather x2, blocking collectives, translate(): return add_piece(lax.all_gather(padded, 'coef', axis=0, tiled=True))  84 us
    all_gather x1, blocking collectives, local(): lax.all_gather(adjoints, 'coef', axis=0, tiled=True)  50 us
    all_gather x1, blocking collectives, local(): lax.all_gather(coupled, 'coef', axis=0, tiled=True)  40.5 us
    unnamed x61, other arithmetic  21.7 us
    all_gather x1, blocking collectives, local(): class_rows = lax.all_gather(tmatrices, 'tiles', axis=0, tiled=True)  19.3 us
    all_to_all x1, starting transfers between devices, local(): lax.all_to_all(class_rows, 'coef', split_axis=2, concat_axis=1, tiled=True)  11.2 us
    ppermute x2, starting transfers between devices, padded_2(): lax.ppermute(head, axis, [((i + 1) % count, i) for i in range(ends)])  7.28 us
    gather x2, local copies, waits for them, and re-layouts, local(): picked = jnp.take(sub_table, classes, axis=0)  6.91 us
  transfers between devices with their start and end apart: 5, of which 1 were waited for; matrix products, arithmetic and copies ran while one was open for 6% of the time, Pallas kernels for 0%

commit v1 on v0

--- a/solution.py
+++ b/solution.py
@@ -43,6 +43,19 @@
     own_first = coef_index * row_count
 
     def translate(source, weight_table, starts, adjoint_mode):
+
+        def deliver_vectors(xs, peer_axis):
+            far_arr = jnp.concatenate(
+                lax.all_to_all(
+                    jnp.stack(lax.axis_size(peer_axis) * [xs]),
+                    axis_name=peer_axis,
+                    split_axis=0,
+                    concat_axis=0,
+                ),
+                0,
+            )
+            return far_arr
+
         padded = padded_2(source, (("tiles", 1),), HW)
         own_mats = lax.dynamic_slice_in_dim(couple, own_first, row_count, 2 if adjoint_mode else 1)
 
@@ -58,7 +71,7 @@
                 "nrk,kni->ri", block_mat, selected, preferred_element_type=jnp.float32
             )
 
-        return add_piece(lax.all_gather(padded, "coef", axis=0, tiled=True))
+        return add_piece(deliver_vectors(padded, "coef"))
 
     coupled = translate(fields, slot_weight, forward_starts, False).astype(jnp.bfloat16)
     class_rows = lax.all_gather(tmatrices, "tiles", axis=0, tiled=True)

time: 261 us -> 205 us (0.79)
  blocking collectives: 194 us -> 113 us
  waiting for transfers between devices: 0.59 us -> 22.4 us
    all_gather x2 -> x0, blocking collectives: 84 us -> none  [translate(): return add_piece(lax.all_gather(padded, 'coef', axis=0, tiled=True))]
    all_to_all x0 -> x2, waiting for transfers between devices: none -> 21.1 us  [deliver_vectors(): lax.all_to_all(jnp.stack(lax.axis_size(peer_axis) * [xs]), axis_name=peer...]
    all_to_all x1, starting transfers between devices: 11.2 us -> 3.57 us  [local(): lax.all_to_all(class_rows, 'coef', split_axis=2, concat_axis=1, tiled=True)]
    all_to_all x0 -> x2, starting transfers between devices: none -> 7.08 us  [deliver_vectors(): lax.all_to_all(jnp.stack(lax.axis_size(peer_axis) * [xs]), axis_name=peer...]
    all_gather x1, blocking collectives: 40.5 us -> 45.6 us  [local(): lax.all_gather(coupled, 'coef', axis=0, tiled=True)]
  transfers between devices with their start and end apart: 5 -> 7, of which waited for: 1 -> 3; matrix products, arithmetic and copies ran while one was open for 6% -> 8% of each run, Pallas kernels for 0% -> 0%
where the time goes in v1:
time: 205 us; the launch traced here: 203 us
  blocking collectives  113 us (55%)
  other arithmetic  24.9 us (12%)
  waiting for transfers between devices  22.4 us (11%)
  starting transfers between devices  21.8 us (11%)
  local copies, waits for them, and re-layouts  15.1 us (7%)
  matrix products  4.25 us (2%)
    all_gather x1, blocking collectives, local(): lax.all_gather(adjoints, 'coef', axis=0, tiled=True)  48.3 us
    all_gather x1, blocking collectives, local(): lax.all_gather(coupled, 'coef', axis=0, tiled=True)  45.6 us
    unnamed x61, other arithmetic  21.7 us
    all_to_all x2, waiting for transfers between devices, deliver_vectors(): lax.all_to_all(jnp.stack(lax.axis_size(peer_axis) * [xs]), axis_name=peer...  21.1 us
    all_gather x1, blocking collectives, local(): class_rows = lax.all_gather(tmatrices, 'tiles', axis=0, tiled=True)  19.2 us
    ppermute x2, starting transfers between devices, padded_2(): lax.ppermute(head, axis, [((i + 1) % count, i) for i in range(ends)])  7.28 us
    all_to_all x2, starting transfers between devices, deliver_vectors(): lax.all_to_all(jnp.stack(lax.axis_size(peer_axis) * [xs]), axis_name=peer...  7.08 us
    gather x2, local copies, waits for them, and re-layouts, local(): picked = jnp.take(sub_table, classes, axis=0)  6.91 us
  transfers between devices with their start and end apart: 7, of which 3 were waited for; matrix products, arithmetic and copies ran while one was open for 8% of the time, Pallas kernels for 0%

profile of v1, /device:TPU:32, one launch (start us, length us, event | category | flops | bytes accessed | tf_op | source)
XLA Modules:
  0.0 202.9 jit_solution(68533548662876610)
XLA Ops:
  0.6 0.8 fusion.138
  1.4 1.9 collective-permute-start
  3.3 3.6 %collective-permute-start.1 = (bf16[16,15]{1,0:T(8,128)(2,1)S(1)}, bf16[16,15]{1,0:T(8,128)(2,1)S(1)}, u32[]{:S(2)}, u32[]{:S(2)}) collective-permute-start(bf16[16,15]{1,0:T(8,128)(2,1)S(1)} %get-tuple-element.37), channel_id=1, source_target_pairs={{16,0},{32,16},{48,32},{64,48},{80,64},{96,80},{112,96},{128,112},... | collective-permute-start | bytes 1448 | tf_op jit(solution)/shard_map/ppermute | solution.py:20
  7.0 0.8 fusion.133
  7.8 19.2 %all_gather.10 = bf16[64,16,256]{2,1,0:T(8,128)(2,1)S(1)} all-gather(bf16[4,16,256]{2,1,0:T(8,128)(2,1)} %param.9), channel_id=1, replica_groups=mesh['tiles'=16,'coef'=16] {'tiles'}, dimensions={0}, use_global_device_ids=true | all-gather | bytes 557056 | tf_op jit(solution)/shard_map/all_gather | solution.py:77
  27.1 48.3 %all_gather.11 = bf16[256,512]{1,0:T(8,128)(2,1)S(1)} all-gather(bf16[16,512]{1,0:T(8,128)(2,1)} %param.7), channel_id=1, replica_groups=mesh['tiles'=16,'coef'=16] {'coef'}, dimensions={0}, use_global_device_ids=true | all-gather | bytes 278528 | tf_op jit(solution)/shard_map/all_gather | solution.py:93
  75.5 0.7 compare_select_fusion
  76.2 0.8 pad_maximum_fusion
  77.0 0.8 stack.224
  77.7 3.5 %all-to-all-start = ((bf16[16,16,542]{2,1,0:T(8,128)(2,1)}), bf16[16,16,542]{2,1,0:T(8,128)(2,1)S(1)}, u32[]{:S(2)}, u32[]{:S(2)}) async-start(bf16[16,16,542]{2,1,0:T(8,128)(2,1)} %stack.224), calls=%async_computation | async-start | bytes 655360 | tf_op jit(solution)/shard_map/all_to_all | solution.py:49
  81.3 1.3 copy.22
  82.6 1.5 reshape.75
  84.1 3.4 %gather_fusion = bf16[512,16,256]{2,1,0:T(8,128)(2,1)} fusion(bf16[64,16,256]{2,1,0:T(8,128)(2,1)S(1)} %all_gather.10, s32[1024]{0:T(1024)S(1)} %pad_clamp_fusion), kind=kCustom, calls=%fused_computation | custom fusion | bytes 8390656 | tf_op jit(solution)/shard_map/jit(_take)/gather | solution.py:79
  87.5 0.2 copy.40
  88.0 6.5 %all-to-all-done = bf16[16,16,542]{2,1,0:T(8,128)(2,1)S(1)} async-done(((bf16[16,16,542]{2,1,0:T(8,128)(2,1)}), bf16[16,16,542]{2,1,0:T(8,128)(2,1)S(1)}, u32[]{:S(2)}, u32[]{:S(2)}) %all-to-all-start) | async-done | bytes 277536 | tf_op jit(solution)/shard_map/all_to_all | solution.py:49
  94.5 3.6 %all-to-all-start.1 = ((bf16[16,2,8192]{2,1,0:T(2,128)(2,1)}), bf16[16,2,8192]{2,1,0:T(2,128)(2,1)S(1)}, u32[]{:S(2)}, u32[]{:S(2)}) async-start(bf16[16,2,8192]{2,1,0:T(2,128)(2,1)} %reshape.75), calls=%async_computation.1 | async-start | bytes 1048576 | tf_op jit(solution)/shard_map/all_to_all | solution.py:87
  102.4 2.1 %fusion.8 = bf16[16,512]{1,0:T(8,128)(2,1)S(1)} fusion(bf16[256,30,512]{2,0,1:T(8,128)(2,1)S(1)} %fusion.73, bf16[30,256,256]{2,1,0:T(8,128)(2,1)} %param.8, s32[]{:T(128)S(6)} %select_n.19), kind=kOutput, calls=%fused_computation.9 | convolution fusion | flops 125837312 | bytes 8126468 | tf_op jit(solution)/shard_map/nrk,kni->ri/dot_general | solution.py:70
  104.4 45.6 %all_gather.9 = bf16[256,512]{1,0:T(8,128)(2,1)S(1)} all-gather(bf16[16,512]{1,0:T(8,128)(2,1)S(1)} %fusion.8), channel_id=1, replica_groups=mesh['tiles'=16,'coef'=16] {'coef'}, dimensions={0}, use_global_device_ids=true | all-gather | bytes 278528 | tf_op jit(solution)/shard_map/all_gather | solution.py:83
  150.1 0.2 copy.39
  150.3 0.7 reshape.76
  151.0 0.3 copy.24
  151.3 1.3 copy.25
  152.6 3.5 %gather_fusion.1 = bf16[512,256,16]{1,2,0:T(8,128)(2,1)} fusion(bf16[64,256,16]{1,2,0:T(8,128)(2,1)S(1)} %copy.25, s32[1024]{0:T(1024)S(1)} %pad_clamp_fusion), kind=kCustom, calls=%fused_computation.1 | custom fusion | bytes 8390656 | tf_op jit(solution)/shard_map/jit(_take)/gather | solution.py:89
  156.1 13.6 %multiply_reduce_fusion = (bf16[512,16]{1,0:T(8,128)(2,1)S(1)}, f32[512,16]{1,0:T(8,128)S(1)}) fusion(f32[512,256]{1,0:T(8,128)S(1)} %copy.40, bf16[512,256,16]{1,2,0:T(8,128)(2,1)} %gather_fusion.1, pred[512]{0:T(512)(128)(4,1)S(1)} %compare_and_fusion, bf16[512,16,256]{2,1,0:T(8,128)(2,1)} %gather_fusion, f32[512,256]{1,0:T(8,128)S(1)} %copy.39), kind=kLoop, calls=%fused_computation.2 | loop fusion | flops 16760832 | bytes 9486848
  169.9 1.9 collective-permute-start.2
  171.8 3.6 %collective-permute-start.3 = (bf16[16,15]{1,0:T(8,128)(2,1)S(1)}, bf16[16,15]{1,0:T(8,128)(2,1)S(1)}, u32[]{:S(2)}, u32[]{:S(2)}) collective-permute-start(bf16[16,15]{1,0:T(8,128)(2,1)S(1)} %get-tuple-element.35), channel_id=1, source_target_pairs={{16,0},{32,16},{48,32},{64,48},{80,64},{96,80},{112,96},{128,112},... | collective-permute-start | bytes 1448 | tf_op jit(solution)/shard_map/ppermute | solution.py:20
  175.4 1.3 collective-permute-done.3
  176.8 0.7 stack.256
  177.6 3.5 %all-to-all-start.2 = ((bf16[16,16,542]{2,1,0:T(8,128)(2,1)}), bf16[16,16,542]{2,1,0:T(8,128)(2,1)S(1)}, u32[]{:S(2)}, u32[]{:S(2)}) async-start(bf16[16,16,542]{2,1,0:T(8,128)(2,1)} %stack.256), calls=%async_computation.2 | async-start | bytes 655360 | tf_op jit(solution)/shard_map/all_to_all | solution.py:49
  181.2 0.6 fusion.134
  181.8 14.6 %all-to-all-done.2 = bf16[16,16,542]{2,1,0:T(8,128)(2,1)S(1)} async-done(((bf16[16,16,542]{2,1,0:T(8,128)(2,1)}), bf16[16,16,542]{2,1,0:T(8,128)(2,1)S(1)}, u32[]{:S(2)}, u32[]{:S(2)}) %all-to-all-start.2) | async-done | bytes 277536 | tf_op jit(solution)/shard_map/all_to_all | solution.py:49
  200.8 2.2 %fusion.9 = bf16[16,512]{1,0:T(8,128)(2,1)} fusion(bf16[256,30,512]{2,0,1:T(8,128)(2,1)S(1)} %fusion.13, bf16[30,256,256]{2,1,0:T(8,128)(2,1)S(1)} %copy-done, s32[]{:T(128)S(6)} %select_n.19, bf16[16,512]{1,0:T(8,128)(2,1)S(1)} %copy-done.2), kind=kOutput, calls=%fused_computation.10 | convolution fusion | flops 125853696 | bytes 9863172 | tf_op jit(solution)/shard_map/nkr,kni->ri/dot_general | solution.py:66
  (82 shorter events, 8.9 us)
Async XLA Ops:
  0.6 87.3 %copy-start.3 = (s32[512]{0:T(512)S(1)}, s32[512]{0:T(512)}, u32[]{:S(2)}) copy-start(s32[512]{0:T(512)} %param.11) | copy-start | bytes 6148
  1.4 74.8 %collective-permute-start = (bf16[16,15]{1,0:T(8,128)(2,1)S(1)}, bf16[16,15]{1,0:T(8,128)(2,1)S(1)}, u32[]{:S(2)}, u32[]{:S(2)}) collective-permute-start(bf16[16,15]{1,0:T(8,128)(2,1)S(1)} %get-tuple-element.36), channel_id=1, source_target_pairs={{0,16},{16,32},{32,48},{48,64},{64,80},{80,96},{96,112},{112,128},... | collective-permute-start | bytes 1448 | tf_op jit(solution)/shard_map/ppermute | solution.py:18
  3.3 72.8 %collective-permute-start.1 = (bf16[16,15]{1,0:T(8,128)(2,1)S(1)}, bf16[16,15]{1,0:T(8,128)(2,1)S(1)}, u32[]{:S(2)}, u32[]{:S(2)}) collective-permute-start(bf16[16,15]{1,0:T(8,128)(2,1)S(1)} %get-tuple-element.37), channel_id=1, source_target_pairs={{16,0},{32,16},{48,32},{64,48},{80,64},{96,80},{112,96},{128,112},... | collective-permute-start | bytes 1448 | tf_op jit(solution)/shard_map/ppermute | solution.py:20
  77.7 16.7 %all-to-all-start = ((bf16[16,16,542]{2,1,0:T(8,128)(2,1)}), bf16[16,16,542]{2,1,0:T(8,128)(2,1)S(1)}, u32[]{:S(2)}, u32[]{:S(2)}) async-start(bf16[16,16,542]{2,1,0:T(8,128)(2,1)} %stack.224), calls=%async_computation | async-start | bytes 655360 | tf_op jit(solution)/shard_map/all_to_all | solution.py:49
  94.5 55.9 %all-to-all-start.1 = ((bf16[16,2,8192]{2,1,0:T(2,128)(2,1)}), bf16[16,2,8192]{2,1,0:T(2,128)(2,1)S(1)}, u32[]{:S(2)}, u32[]{:S(2)}) async-start(bf16[16,2,8192]{2,1,0:T(2,128)(2,1)} %reshape.75), calls=%async_computation.1 | async-start | bytes 1048576 | tf_op jit(solution)/shard_map/all_to_all | solution.py:87
  156.1 25.1 %copy-start.1 = (bf16[16,512]{1,0:T(8,128)(2,1)S(1)}, bf16[16,512]{1,0:T(8,128)(2,1)}, u32[]{:S(2)}) copy-start(bf16[16,512]{1,0:T(8,128)(2,1)} %param.6) | copy-start | bytes 49156
  169.9 5.6 %collective-permute-start.2 = (bf16[16,15]{1,0:T(8,128)(2,1)S(1)}, bf16[16,15]{1,0:T(8,128)(2,1)S(1)}, u32[]{:S(2)}, u32[]{:S(2)}) collective-permute-start(bf16[16,15]{1,0:T(8,128)(2,1)S(1)} %get-tuple-element.34), channel_id=1, source_target_pairs={{0,16},{16,32},{32,48},{48,64},{64,80},{80,96},{96,112},{112,128},... | collective-permute-start | bytes 1448 | tf_op jit(solution)/shard_map/ppermute | solution.py:18
  171.8 5.0 %collective-permute-start.3 = (bf16[16,15]{1,0:T(8,128)(2,1)S(1)}, bf16[16,15]{1,0:T(8,128)(2,1)S(1)}, u32[]{:S(2)}, u32[]{:S(2)}) collective-permute-start(bf16[16,15]{1,0:T(8,128)(2,1)S(1)} %get-tuple-element.35), channel_id=1, source_target_pairs={{16,0},{32,16},{48,32},{64,48},{80,64},{96,80},{112,96},{128,112},... | collective-permute-start | bytes 1448 | tf_op jit(solution)/shard_map/ppermute | solution.py:20
  177.6 18.8 %all-to-all-start.2 = ((bf16[16,16,542]{2,1,0:T(8,128)(2,1)}), bf16[16,16,542]{2,1,0:T(8,128)(2,1)S(1)}, u32[]{:S(2)}, u32[]{:S(2)}) async-start(bf16[16,16,542]{2,1,0:T(8,128)(2,1)} %stack.256), calls=%async_computation.2 | async-start | bytes 655360 | tf_op jit(solution)/shard_map/all_to_all | solution.py:49
  196.4 4.3 %copy-start = (bf16[30,256,256]{2,1,0:T(8,128)(2,1)S(1)}, bf16[30,256,256]{2,1,0:T(8,128)(2,1)}, u32[]{:S(2)}) copy-start(bf16[30,256,256]{2,1,0:T(8,128)(2,1)} %param.8) | copy-start | bytes 11796484
  196.4 4.3 %copy-start.2 = (bf16[16,512]{1,0:T(8,128)(2,1)S(1)}, bf16[16,512]{1,0:T(8,128)(2,1)}, u32[]{:S(2)}) copy-start(bf16[16,512]{1,0:T(8,128)(2,1)} %param.7) | copy-start | bytes 49156
